TPU v7x, 32 devices: a whole 2x2x4 slice. The times are simulated.
32 devices in a mesh: req: 8 (over z, y), ctx: 4 (over x, core).
Axes of the slice: x: 2, y: 2, z: 4, core: 2. Of those that a mesh axis runs over, the one named last changes fastest.
Arguments:
- history: bfloat16 [24576, 1024], P(('req', 'ctx')), may hold values from -6 to 6
- block_owner: int32 [1536, 1], P(('req', 'ctx')), may hold values from 0 to 7; in each aligned block of 48 rows (0 to 47, 48 to 95, ...) at most 12 rows name the same one
- candidates: bfloat16 [4096, 1024], P(('req', 'ctx')), may hold values from -6 to 6
- w_kv: bfloat16 [1024, 2048], replicated, may hold values from -0.1875 to 0.1875
- w_qu: bfloat16 [1024, 2048], replicated, may hold values from -0.1875 to 0.1875
- w_out: bfloat16 [1024, 1024], replicated, may hold values from -0.1875 to 0.1875
Outputs:
- scored: bfloat16 [4096, 1024], P(('req', 'ctx'))
Inputs may be any that keep to these rules, and one draw needn't show every extreme that they name: `block_owner`: each packed block belongs to one request; among the 48 blocks of one device at most 12 belong to the same request, and that most is reached on some device; every request owns at least one block.
All inputs are finite; a program needn't handle non-finite values.
Results may differ from a plain program's by a relative error of at most 0.0052.
Values may be sent and summed in bfloat16 or wider, within the bound.
No kernel may reach another device: no remote copies, remote signals or barrier semaphores. Data moves between devices by JAX's collectives and lax.ppermute only.
A program may use at most 128 MiB of HBM per device.

v0:
```python
import jax
import jax.numpy as jnp
from jax import lax
from jax.sharding import PartitionSpec as P

HEAD = 128
key_span = 512


def attend(queries, keys_values):
    count, width = queries.shape
    heads = width // HEAD
    rows = keys_values.shape[0]
    query = queries.reshape(count, heads, HEAD)
    pieces = keys_values.reshape(rows // key_span, key_span, 2, heads, HEAD)
    factor = HEAD ** (-0.5)

    def add_block(total, piece):
        scores = (
            jnp.einsum("qhd,khd->hqk", query, piece[:, 0], preferred_element_type=jnp.float32)
            * factor
        )
        weights = jax.nn.silu(scores).astype(jnp.bfloat16)
        return (
            total
            + jnp.einsum("hqk,khd->qhd", weights, piece[:, 1], preferred_element_type=jnp.float32),
            None,
        )

    total, _ = lax.scan(add_block, jnp.zeros((count, heads, HEAD), jnp.float32), pieces)
    return total.reshape(count, width)


def on_device(history, block_owner, candidates, w_kv, w_qu, w_out):
    owners_count = lax.axis_size("req")
    rows, width = history.shape
    blocks = block_owner.shape[0]
    events = rows // blocks
    capacity = 2 * blocks // owners_count
    owner = block_owner[:, 0]
    onehot = (owner[:, None] == jnp.arange(owners_count, dtype=jnp.int32)[None, :]).astype(
        jnp.int32
    )
    rank = jnp.sum((jnp.cumsum(onehot, axis=0) - onehot) * onehot, axis=1)
    slot = owner * capacity + rank
    placing = (
        slot[None, :] == jnp.arange(owners_count * capacity, dtype=jnp.int32)[:, None]
    ).astype(jnp.bfloat16)
    packed = jnp.dot(
        placing, history.reshape(blocks, events * width), preferred_element_type=jnp.float32
    )
    packed = packed.astype(jnp.bfloat16).reshape(owners_count, capacity, events, width)
    raw = lax.all_to_all(packed, "req", split_axis=0, concat_axis=0, tiled=True)
    flat = raw.reshape(-1, raw.shape[-1])
    linear = jnp.dot(flat, w_kv, preferred_element_type=jnp.float32)
    half = linear.shape[-1] // 2
    made = jnp.concatenate([jax.nn.silu(linear[:, :half]), linear[:, half:]], axis=1).astype(
        jnp.bfloat16
    )
    arrived = made.reshape(raw.shape[:-1] + (made.shape[-1],))
    context = arrived.reshape(-1, 2 * width)
    projected = jnp.dot(candidates, w_qu, preferred_element_type=jnp.float32)
    queries = jax.nn.silu(projected[:, :width]).astype(jnp.bfloat16)
    gate = jax.nn.silu(projected[:, width:])
    partial_value = attend(lax.all_gather(queries, "ctx", axis=0, tiled=True), context)
    attended = lax.psum_scatter(partial_value, "ctx", scatter_dimension=0, tiled=True)
    mean = jnp.mean(attended, axis=-1, keepdims=True)
    centred = attended - mean
    variance = jnp.mean(centred * centred, axis=-1, keepdims=True)
    mixed = (centred * lax.rsqrt(variance + 1e-05) * gate).astype(jnp.bfloat16)
    result = candidates.astype(jnp.float32) + jnp.dot(
        mixed, w_out, preferred_element_type=jnp.float32
    )
    return result.astype(jnp.bfloat16)


def solution(mesh):
    placed = (
        P(("req", "ctx"), None),
        P(("req", "ctx"), None),
        P(("req", "ctx"), None),
        P(),
        P(),
        P(),
    )
    return jax.shard_map(
        on_device, mesh=mesh, in_specs=placed, out_specs=P(("req", "ctx"), None), check_vma=False
    )
```

profile of v0, /device:TPU:0, one launch (start us, length us, event | category | flops | bytes accessed | tf_op | source)
XLA Modules:
  0.0 196.9 jit_solution(2472412631401539334)
XLA Ops:
  6.5 0.9 fusion.17
  7.5 0.8 select_reduce_fusion
  8.3 0.7 multiply_add_fusion
  9.0 3.8 %reshape.37 = bf16[48,16384]{1,0:T(8,128)(2,1)} reshape(bf16[768,1024]{1,0:T(8,128)(2,1)} %param.8) | data formatting | bytes 3145728 | tf_op jit(solution)/shard_map/reshape | solution.py:50
  12.8 2.4 %convolution_convert_fusion = bf16[96,16384]{1,0:T(8,128)(2,1)S(1)} fusion(bf16[48,16384]{1,0:T(8,128)(2,1)} %reshape.37, s32[48]{0:T(128)S(1)} %multiply_add_fusion), kind=kOutput, calls=%fused_computation.15 | convolution fusion | flops 152572416 | bytes 4718784 | tf_op jit(solution)/shard_map/dot_general | solution.py:49
  15.1 3.7 %copy.17 = bf16[12,8,16,1024]{3,2,1,0:T(8,128)(2,1)} copy(bf16[12,8,16,1024]{3,1,2,0:T(8,128)(2,1)S(1)} %bitcast.66) | data formatting | bytes 6291456
  18.8 7.4 %all-to-all-start = ((bf16[8,12,16,1024]{3,2,1,0:T(8,128)(2,1)}), bf16[8,12,16,1024]{3,2,1,0:T(8,128)(2,1)}, u32[]{:S(2)}, u32[]{:S(2)}) async-start(bf16[8,12,16,1024]{3,2,1,0:T(8,128)(2,1)} %bitcast.65), calls=%async_computation | async-start | bytes 6291456 | tf_op jit(solution)/shard_map/all_to_all | solution.py:53
  26.3 2.9 %fusion.20 = f32[128,2048]{1,0:T(8,128)S(1)} fusion(bf16[128,1024]{1,0:T(8,128)(2,1)S(1)} %copy-done.1, bf16[1024,2048]{1,0:T(8,128)(2,1)} %param.12), kind=kOutput, calls=%fused_computation.38 | convolution fusion | flops 536870912 | bytes 5505024 | tf_op jit(solution)/shard_map/dot_general | solution.py:62
  29.2 0.8 multiply_convert_fusion.2
  30.1 18.2 %all-gather.2.cloned.1.call-done = bf16[512,1024]{1,0:T(8,128)(2,1)} async-done(((bf16[128,1024]{1,0:T(8,128)(2,1)}), bf16[512,1024]{1,0:T(8,128)(2,1)}) %all-gather.2.cloned.1.call-update) | async-done | bytes 1048592 | tf_op jit(solution)/shard_map/all_gather | solution.py:65
  48.3 2.4 %copy_bitcast_fusion.1 = bf16[512,8,128]{2,0,1:T(8,128)(2,1)} fusion(bf16[512,1024]{1,0:T(8,128)(2,1)} %all-gather.2.cloned.1.call-done), kind=kLoop, calls=%fused_computation.21 | loop fusion | bytes 2097152
  50.7 46.4 %all-to-all-done = bf16[8,12,16,1024]{3,2,1,0:T(8,128)(2,1)} async-done(((bf16[8,12,16,1024]{3,2,1,0:T(8,128)(2,1)}), bf16[8,12,16,1024]{3,2,1,0:T(8,128)(2,1)}, u32[]{:S(2)}, u32[]{:S(2)}) %all-to-all-start) | async-done | bytes 3145760 | tf_op jit(solution)/shard_map/all_to_all | solution.py:53
  97.0 9.5 %fusion.19 = f32[1536,2048]{1,0:T(8,128)S(1)} fusion(bf16[1536,1024]{1,0:T(8,128)(2,1)} %bitcast.1, bf16[1024,2048]{1,0:T(8,128)(2,1)} %param.11), kind=kOutput, calls=%fused_computation.37 | convolution fusion | flops 6442450944 | bytes 19922944 | tf_op jit(solution)/shard_map/dot_general | solution.py:55
  106.6 2.9 %multiply_convert_fusion = bf16[1536,1024]{1,0:T(8,128)(2,1)} fusion(f32[1536,2048]{1,0:T(8,128)S(1)} %fusion.19), kind=kLoop, calls=%fused_computation.18 | loop fusion | flops 7864320 | bytes 9437184 | tf_op jit(solution)/shard_map/convert
  109.5 0.5 slice.41
  110.0 3.9 %maximum_bitcast_fusion = bf16[192,8,16,128]{3,1,2,0:T(8,128)(2,1)S(1)} fusion(bf16[1536,1024]{1,0:T(8,128)(2,1)S(1)} %slice.41, bf16[1536,1024]{1,0:T(8,128)(2,1)} %multiply_convert_fusion), kind=kLoop, calls=%fused_computation.17 | loop fusion | flops 12582912 | bytes 12582912
  113.9 5.0 %copy.18 = bf16[192,8,16,128]{3,2,1,0:T(8,128)(2,1)} copy(bf16[192,8,16,128]{3,1,2,0:T(8,128)(2,1)S(1)} %maximum_bitcast_fusion) | data formatting | bytes 12582912
  118.9 33.1 %while.11 = (s32[]{:T(128)}, f32[512,8,128]{0,2,1:T(8,128)}, bf16[3,512,2,8,128]{4,3,2,1,0:T(8,128)(2,1)}, bf16[512,8,128]{2,0,1:T(8,128)(2,1)}, s32[]{:T(128)}, /*index=5*/s32[]{:T(128)}) while((s32[]{:T(128)}, f32[512,8,128]{0,2,1:T(8,128)}, bf16[3,512,2,8,128]{4,3,2,1,0:T(8,128)(2,1)}, bf16[512,8,128]{2,0,1:T(8,128)(2,1)}, ...), condition=%wide.region_3.4_spmd.clone, body=%wide.region_2.3_spmd.clone.sunk | while | flops 1087373312 | bytes 15728723 | solution.py:30
  118.9 2.0 constant_dynamic-slice_fusion.2
  120.9 1.9 copy.23
  122.8 6.7 %bitcast_add_fusion.2 = f32[512,8,128]{0,2,1:T(8,128)} fusion(f32[512,8,128]{0,2,1:T(8,128)} %get-tuple-element.87, bf16[512,8,128]{2,0,1:T(8,128)(2,1)} %get-tuple-element.95, bf16[512,2,8,128]{3,0,2,1:T(8,128)(2,1)} %bitcast.63, pred[]{:T(512)S(6)} %compare.3), kind=kOutput, calls=%fused_computation.9.clone.1 | convolution fusion | flops 1087373312 | bytes 7340033 | tf_op jit(solution)/shard_map/while/body/eval_jaxpr/hqk,khd->qhd/dot_general | solution.py:26
  129.5 2.0 constant_dynamic-slice_fusion.2
  131.4 1.9 copy.23
  133.3 7.4 %bitcast_add_fusion.2 = f32[512,8,128]{0,2,1:T(8,128)} fusion(f32[512,8,128]{0,2,1:T(8,128)} %get-tuple-element.87, bf16[512,8,128]{2,0,1:T(8,128)(2,1)} %get-tuple-element.95, bf16[512,2,8,128]{3,0,2,1:T(8,128)(2,1)} %bitcast.63, pred[]{:T(512)S(6)} %compare.3), kind=kOutput, calls=%fused_computation.9.clone.1 | convolution fusion | flops 1087373312 | bytes 7340033 | tf_op jit(solution)/shard_map/while/body/eval_jaxpr/hqk,khd->qhd/dot_general | solution.py:26
  140.7 2.0 constant_dynamic-slice_fusion.2
  142.7 1.9 copy.23
  144.6 7.4 %bitcast_add_fusion.2 = f32[512,8,128]{0,2,1:T(8,128)} fusion(f32[512,8,128]{0,2,1:T(8,128)} %get-tuple-element.87, bf16[512,8,128]{2,0,1:T(8,128)(2,1)} %get-tuple-element.95, bf16[512,2,8,128]{3,0,2,1:T(8,128)(2,1)} %bitcast.63, pred[]{:T(512)S(6)} %compare.3), kind=kOutput, calls=%fused_computation.9.clone.1 | convolution fusion | flops 1087373312 | bytes 7340033 | tf_op jit(solution)/shard_map/while/body/eval_jaxpr/hqk,khd->qhd/dot_general | solution.py:26
  152.0 2.9 %copy.14 = f32[512,1024]{1,0:T(8,128)} copy(f32[512,1024]{0,1:T(8,128)} %bitcast.67) | data formatting | bytes 4194304 | tf_op jit(solution)/shard_map/reshape | solution.py:31
  154.9 30.4 %reduce-scatter.2.cloned.1.call-done = f32[128,1024]{1,0:T(8,128)} async-done(((f32[512,1024]{1,0:T(8,128)}), f32[128,1024]{1,0:T(8,128)}) %reduce-scatter.2.cloned.1.call-update) | async-done | bytes 524304 | tf_op jit(solution)/shard_map/reduce_scatter | solution.py:66
  185.3 1.2 reduce_sum.28
  186.5 1.2 multiply_reduce_fusion
  187.7 2.3 %fusion.12 = bf16[128,1024]{1,0:T(8,128)(2,1)} fusion(bf16[1024,1024]{1,0:T(8,128)(2,1)S(1)} %copy-done, bf16[128,1024]{1,0:T(8,128)(2,1)S(1)} %copy-done.1, f32[128,2048]{1,0:T(8,128)S(1)} %fusion.20, f32[128,1024]{1,0:T(8,128)} %reduce-scatter.2.cloned.1.call-done, f32[128]{0:T(128)S(1)} %add_rsqrt_fusion, f32[128]{0:T(128)S(1)} %broadcast_multiply_fusion), kind=kOutput, calls=%fused_computation.20 | convolution fusion | flops 269877248 | bytes 3671040 | tf_op jit(solution)/shard_map/dot_general | solution.py:71
  (12 shorter events, 0.2 us)
Async XLA Ops:
  6.5 181.2 %copy-start = (bf16[1024,1024]{1,0:T(8,128)(2,1)S(1)}, bf16[1024,1024]{1,0:T(8,128)(2,1)}, u32[]{:S(2)}) copy-start(bf16[1024,1024]{1,0:T(8,128)(2,1)} %param.13) | copy-start | bytes 6291460
  18.8 7.5 %copy-start.1 = (bf16[128,1024]{1,0:T(8,128)(2,1)S(1)}, bf16[128,1024]{1,0:T(8,128)(2,1)}, u32[]{:S(2)}) copy-start(bf16[128,1024]{1,0:T(8,128)(2,1)} %param.10) | copy-start | bytes 786436
  18.8 78.3 %all-to-all-start = ((bf16[8,12,16,1024]{3,2,1,0:T(8,128)(2,1)}), bf16[8,12,16,1024]{3,2,1,0:T(8,128)(2,1)}, u32[]{:S(2)}, u32[]{:S(2)}) async-start(bf16[8,12,16,1024]{3,2,1,0:T(8,128)(2,1)} %bitcast.65), calls=%async_computation | async-start | bytes 6291456 | tf_op jit(solution)/shard_map/all_to_all | solution.py:53
  26.2 22.1 %all-gather.2.cloned.1.call-start = ((), (), s32[]{:S(2)}) async-start(), calls=%async_computation.2 | async-start | bytes 1310720 | tf_op jit(solution)/shard_map/all_gather | solution.py:65
  30.1 155.2 %reduce-scatter.2.cloned.1.call-start = ((), (), s32[]{:S(2)}) async-start(), calls=%async_computation.3 | async-start | bytes 2621440 | tf_op jit(solution)/shard_map/reduce_scatter | solution.py:66
Sparse Core Ops, SparseCore 0:
  30.2 18.0 all-gather.1
  155.1 30.1 reduce-scatter.1
where the time goes:
time: 198 us; the launch traced here: 197 us
  waiting for transfers between devices  94.9 us (48%)
  matrix products  38.5 us (19%)
  local copies, waits for them, and re-layouts  29.9 us (15%)
  between operations  13.5 us (7%)
  other arithmetic  12.5 us (6%)
  starting transfers between devices  7.52 us (4%)
    all_to_all x1, waiting for transfers between devices, on_device(): raw = lax.all_to_all(packed, 'req', split_axis=0, concat_axis=0, tiled=True)  46.4 us
    reduce_scatter x1, waiting for transfers between devices, on_device(): lax.psum_scatter(partial_value, 'ctx', scatter_dimension=0, tiled=True)  30.4 us
    dot_general x3, matrix products, add_block(): jnp.einsum('hqk,khd->qhd', weights, piece[:, 1], preferred_element_type=j...  21.4 us
    all_gather x1, waiting for transfers between devices, on_device(): lax.all_gather(queries, 'ctx', axis=0, tiled=True)  18.2 us
    dynamic_slice x6, local copies, waits for them, and re-layouts, attend(): lax.scan(add_block, jnp.zeros((count, heads, HEAD), jnp.float32), pieces)  11.7 us
    unnamed x7, local copies, waits for them, and re-layouts  11.1 us
    dot_general x1, matrix products, on_device(): linear = jnp.dot(flat, w_kv, preferred_element_type=jnp.float32)  9.53 us
    all_to_all x1, starting transfers between devices, on_device(): raw = lax.all_to_all(packed, 'req', split_axis=0, concat_axis=0, tiled=True)  7.44 us
  transfers between devices with their start and end apart: 3, of which 3 were waited for; matrix products, arithmetic and copies ran while one was open for 3% of the time, Pallas kernels for 0%

commit v1 on v0

--- a/solution.py
+++ b/solution.py
@@ -5,6 +5,18 @@
 
 HEAD = 128
 key_span = 512
+
+
+def in_blocks(x, dim, size):
+    shape = x.shape
+    tiles = x.reshape(*shape[:dim], size, shape[dim] // size, *shape[dim + 1 :])
+    return jnp.moveaxis(tiles, dim, 0)
+
+
+def joined_along(pieces, dim):
+    shape = list(pieces.shape[1:])
+    shape[dim] *= pieces.shape[0]
+    return jnp.moveaxis(pieces, 0, dim).reshape(shape)
 
 
 def attend(queries, keys_values):
@@ -50,7 +62,14 @@
         placing, history.reshape(blocks, events * width), preferred_element_type=jnp.float32
     )
     packed = packed.astype(jnp.bfloat16).reshape(owners_count, capacity, events, width)
-    raw = lax.all_to_all(packed, "req", split_axis=0, concat_axis=0, tiled=True)
+    devices, here = (lax.axis_size("req"), lax.axis_index("req"))
+    parts = in_blocks(packed, 0, devices)
+    outs = [parts[here]]
+    for step in range(1, devices):
+        sent = parts[here ^ step]
+        outs.append(lax.ppermute(sent, "req", [(i, i ^ step) for i in range(devices)]))
+    parts = jnp.stack(outs)[here ^ jnp.arange(devices)]
+    raw = joined_along(parts, 0)
     flat = raw.reshape(-1, raw.shape[-1])
     linear = jnp.dot(flat, w_kv, preferred_element_type=jnp.float32)
     half = linear.shape[-1] // 2

time: 198 us -> 207 us (1.045)
  local copies, waits for them, and re-layouts: 29.9 us -> 47.3 us
  waiting for transfers between devices: 94.9 us -> 82.7 us
  starting transfers between devices: 7.52 us -> 13.7 us
  matrix products: 38.5 us -> 36.3 us
    all_to_all x1 -> x0, waiting for transfers between devices: 46.4 us -> none  [on_device(): raw = lax.all_to_all(packed, 'req', split_axis=0, concat_axis=0, tiled=True)]
    ppermute x0 -> x7, waiting for transfers between devices: none -> 38.7 us  [on_device(): lax.ppermute(sent, 'req', [(i, i ^ step) for i in range(devices)])]
    all_gather x1, waiting for transfers between devices: 18.2 us -> 0.01 us  [on_device(): lax.all_gather(queries, 'ctx', axis=0, tiled=True)]
    reduce_scatter x1, waiting for transfers between devices: 30.4 us -> 44 us  [on_device(): lax.psum_scatter(partial_value, 'ctx', scatter_dimension=0, tiled=True)]
    ppermute x0 -> x7, starting transfers between devices: none -> 13.6 us  [on_device(): lax.ppermute(sent, 'req', [(i, i ^ step) for i in range(devices)])]
    unnamed x7 -> x17, local copies, waits for them, and re-layouts: 11.1 us -> 19.8 us
    all_to_all x1 -> x0, starting transfers between devices: 7.44 us -> none  [on_device(): raw = lax.all_to_all(packed, 'req', split_axis=0, concat_axis=0, tiled=True)]
    gather x0 -> x1, local copies, waits for them, and re-layouts: none -> 4.31 us  [on_device(): parts = jnp.stack(outs)[here ^ jnp.arange(devices)]]
  transfers between devices with their start and end apart: 3 -> 9, of which waited for: 3 -> 5; matrix products, arithmetic and copies ran while one was open for 3% -> 18% of each run, Pallas kernels for 0% -> 0%
where the time goes in v1:
time: 207 us; the launch traced here: 206 us
  waiting for transfers between devices  82.7 us (40%)
  local copies, waits for them, and re-layouts  47.3 us (23%)
  matrix products  36.3 us (18%)
  starting transfers between devices  13.7 us (7%)
  between operations  13.5 us (7%)
  other arithmetic  12.5 us (6%)
    reduce_scatter x1, waiting for transfers between devices, on_device(): lax.psum_scatter(partial_value, 'ctx', scatter_dimension=0, tiled=True)  44 us
    ppermute x7, waiting for transfers between devices, on_device(): lax.ppermute(sent, 'req', [(i, i ^ step) for i in range(devices)])  38.7 us
    dot_general x3, matrix products, add_block(): jnp.einsum('hqk,khd->qhd', weights, piece[:, 1], preferred_element_type=j...  21.4 us
    unnamed x17, local copies, waits for them, and re-layouts  19.8 us
    ppermute x7, starting transfers between devices, on_device(): lax.ppermute(sent, 'req', [(i, i ^ step) for i in range(devices)])  13.6 us
    dynamic_slice x6, local copies, waits for them, and re-layouts, attend(): lax.scan(add_block, jnp.zeros((count, heads, HEAD), jnp.float32), pieces)  11.5 us
    dot_general x1, matrix products, on_device(): linear = jnp.dot(flat, w_kv, preferred_element_type=jnp.float32)  9.53 us
    gather x1, local copies, waits for them, and re-layouts, on_device(): parts = jnp.stack(outs)[here ^ jnp.arange(devices)]  4.31 us
  transfers between devices with their start and end apart: 9, of which 5 were waited for; matrix products, arithmetic and copies ran while one was open for 18% of the time, Pallas kernels for 0%

profile of v1, /device:TPU:0, one launch (start us, length us, event | category | flops | bytes accessed | tf_op | source)
XLA Modules:
  0.0 206.1 jit_solution(2067396917091008070)
XLA Ops:
  9.0 3.8 %reshape.47 = bf16[48,16384]{1,0:T(8,128)(2,1)} reshape(bf16[768,1024]{1,0:T(8,128)(2,1)} %param.8) | data formatting | bytes 3145728 | tf_op jit(solution)/shard_map/reshape | solution.py:62
  12.8 2.4 %convolution_convert_fusion = bf16[96,16384]{1,0:T(8,128)(2,1)S(1)} fusion(bf16[48,16384]{1,0:T(8,128)(2,1)} %reshape.47, s32[48]{0:T(128)S(1)} %multiply_add_fusion), kind=kOutput, calls=%fused_computation.16 | convolution fusion | flops 152572416 | bytes 4718784 | tf_op jit(solution)/shard_map/dot_general | solution.py:61
  15.1 3.6 %copy.17 = bf16[12,8,16,1024]{3,2,1,0:T(8,128)(2,1)} copy(bf16[12,8,16,1024]{3,1,2,0:T(8,128)(2,1)S(1)} %bitcast.97) | data formatting | bytes 6291456
  18.8 3.7 %dynamic-slice_bitcast_fusion = (bf16[1,12,16,1024]{3,2,1,0:T(8,128)(2,1)}, bf16[1,12,16,1024]{3,2,1,0:T(8,128)(2,1)}, bf16[1,12,16,1024]{3,2,1,0:T(8,128)(2,1)}...) fusion(bf16[8,1,12,16,1024]{4,3,2,0,1:T(8,128)(2,1)} %bitcast.9, ...), kind=kLoop, calls=%fused_computation.33 | loop fusion | bytes 6291488 | tf_op jit(solution)/shard_map/squeeze | solution.py:69
  22.5 3.0 %collective-permute-start = (bf16[1,12,16,1024]{3,2,1,0:T(8,128)(2,1)}, bf16[1,12,16,1024]{3,2,1,0:T(8,128)(2,1)}, u32[]{:S(2)}, u32[]{:S(2)}) collective-permute-start(bf16[1,12,16,1024]{3,2,1,0:T(8,128)(2,1)} %get-tuple-element.61), channel_id=1, source_target_pairs={{0,4},{4,0},{8,12},{12,8},{16,20},{20,16},{24,28},{28,24},{1,5},{5... | collective-permute-start | bytes 1179656 | tf_op jit(solution)/shard_map/ppermute | solution.py:70
  27.0 3.0 %collective-permute-start.3 = (bf16[1,12,16,1024]{3,2,1,0:T(8,128)(2,1)}, bf16[1,12,16,1024]{3,2,1,0:T(8,128)(2,1)}, u32[]{:S(2)}, u32[]{:S(2)}) collective-permute-start(bf16[1,12,16,1024]{3,2,1,0:T(8,128)(2,1)} %get-tuple-element.58), channel_id=1, source_target_pairs={{0,16},{4,20},{8,24},{12,28},{16,0},{20,4},{24,8},{28,12},{1,17},{... | collective-permute-start | bytes 1179656 | tf_op jit(solution)/shard_map/ppermute | solution.py:70
  33.0 1.9 collective-permute-done
  34.9 3.8 %collective-permute-start.5 = (bf16[1,12,16,1024]{3,2,1,0:T(8,128)(2,1)}, bf16[1,12,16,1024]{3,2,1,0:T(8,128)(2,1)S(1)}, u32[]{:S(2)}, u32[]{:S(2)}) collective-permute-start(bf16[1,12,16,1024]{3,2,1,0:T(8,128)(2,1)} %get-tuple-element.56), channel_id=1, source_target_pairs={{0,24},{4,28},{8,16},{12,20},{16,8},{20,12},{24,0},{28,4},{1,25},{... | collective-permute-start | bytes 1179656 | tf_op jit(solution)/shard_map/ppermute | solution.py:70
  38.7 1.8 bitcast_dynamic-update-slice_fusion.6
  40.5 13.2 %collective-permute-done.1 = bf16[1,12,16,1024]{3,2,1,0:T(8,128)(2,1)} collective-permute-done((bf16[1,12,16,1024]{3,2,1,0:T(8,128)(2,1)}, bf16[1,12,16,1024]{3,2,1,0:T(8,128)(2,1)}, u32[]{:S(2)}, u32[]{:S(2)}) %collective-permute-start.1) | collective-permute-done | bytes 393248 | tf_op jit(solution)/shard_map/ppermute | solution.py:70
  56.4 3.4 %collective-permute-done.2 = bf16[1,12,16,1024]{3,2,1,0:T(8,128)(2,1)} collective-permute-done((bf16[1,12,16,1024]{3,2,1,0:T(8,128)(2,1)}, bf16[1,12,16,1024]{3,2,1,0:T(8,128)(2,1)}, u32[]{:S(2)}, u32[]{:S(2)}) %collective-permute-start.2) | collective-permute-done | bytes 393248 | tf_op jit(solution)/shard_map/ppermute | solution.py:70
  59.8 1.8 bitcast_dynamic-update-slice_fusion.4
  63.4 20.2 %collective-permute-done.4 = bf16[1,12,16,1024]{3,2,1,0:T(8,128)(2,1)S(1)} collective-permute-done((bf16[1,12,16,1024]{3,2,1,0:T(8,128)(2,1)}, bf16[1,12,16,1024]{3,2,1,0:T(8,128)(2,1)S(1)}, u32[]{:S(2)}, u32[]{:S(2)}) %collective-permute-start.4) | collective-permute-done | bytes 393248 | tf_op jit(solution)/shard_map/ppermute | solution.py:70
  86.0 4.3 %gather_fusion = bf16[8,12,16,1024]{3,2,1,0:T(8,128)(2,1)} fusion(bf16[8,12,16,1024]{3,2,1,0:T(8,128)(2,1)} %bitcast.99, s32[1024]{0:T(1024)S(1)} %pad_clamp_fusion), kind=kCustom, calls=%fused_computation | custom fusion | bytes 6291488 | tf_op jit(solution)/shard_map/gather | solution.py:71
  90.3 9.5 %fusion.20 = f32[1536,2048]{1,0:T(8,128)S(1)} fusion(bf16[1536,1024]{1,0:T(8,128)(2,1)} %bitcast.100, bf16[1024,2048]{1,0:T(8,128)(2,1)} %param.11), kind=kOutput, calls=%fused_computation.56 | convolution fusion | flops 6442450944 | bytes 19922944 | tf_op jit(solution)/shard_map/dot_general | solution.py:74
  100.4 2.9 %multiply_convert_fusion = bf16[1536,1024]{1,0:T(8,128)(2,1)} fusion(f32[1536,2048]{1,0:T(8,128)S(1)} %fusion.20), kind=kLoop, calls=%fused_computation.19 | loop fusion | flops 7864320 | bytes 9437184 | tf_op jit(solution)/shard_map/convert
  103.3 3.9 %maximum_bitcast_fusion = bf16[192,8,16,128]{3,1,2,0:T(8,128)(2,1)S(1)} fusion(bf16[1536,1024]{1,0:T(8,128)(2,1)S(1)} %slice.43, bf16[1536,1024]{1,0:T(8,128)(2,1)} %multiply_convert_fusion), kind=kLoop, calls=%fused_computation.18 | loop fusion | flops 12582912 | bytes 12582912
  107.2 5.0 %copy.18 = bf16[192,8,16,128]{3,2,1,0:T(8,128)(2,1)} copy(bf16[192,8,16,128]{3,1,2,0:T(8,128)(2,1)S(1)} %maximum_bitcast_fusion) | data formatting | bytes 12582912
  112.2 2.4 %copy_bitcast_fusion.1 = bf16[512,8,128]{2,0,1:T(8,128)(2,1)} fusion(bf16[512,1024]{1,0:T(8,128)(2,1)} %all-gather.2.cloned.1.call-done), kind=kLoop, calls=%fused_computation.22 | loop fusion | bytes 2097152
  114.6 32.9 %while.11 = (s32[]{:T(128)}, f32[512,8,128]{0,2,1:T(8,128)}, bf16[3,512,2,8,128]{4,3,2,1,0:T(8,128)(2,1)}, bf16[512,8,128]{2,0,1:T(8,128)(2,1)}, s32[]{:T(128)}, /*index=5*/s32[]{:T(128)}) while((s32[]{:T(128)}, f32[512,8,128]{0,2,1:T(8,128)}, bf16[3,512,2,8,128]{4,3,2,1,0:T(8,128)(2,1)}, bf16[512,8,128]{2,0,1:T(8,128)(2,1)}, ...), condition=%wide.region_3.4_spmd.clone, body=%wide.region_2.3_spmd.clone.sunk | while | flops 1087373312 | bytes 15728723 | solution.py:42
  114.6 2.0 constant_dynamic-slice_fusion.2
  116.5 1.9 copy.23
  118.4 6.7 %bitcast_add_fusion.2 = f32[512,8,128]{0,2,1:T(8,128)} fusion(f32[512,8,128]{0,2,1:T(8,128)} %get-tuple-element.95, bf16[512,8,128]{2,0,1:T(8,128)(2,1)} %get-tuple-element.103, bf16[512,2,8,128]{3,0,2,1:T(8,128)(2,1)} %bitcast.95, pred[]{:T(512)S(6)} %compare.3), kind=kOutput, calls=%fused_computation.10.clone.1 | convolution fusion | flops 1087373312 | bytes 7340033 | tf_op jit(solution)/shard_map/while/body/eval_jaxpr/hqk,khd->qhd/dot_general | solution.py:38
  125.1 2.0 constant_dynamic-slice_fusion.2
  127.1 1.9 copy.23
  129.0 7.4 %bitcast_add_fusion.2 = f32[512,8,128]{0,2,1:T(8,128)} fusion(f32[512,8,128]{0,2,1:T(8,128)} %get-tuple-element.95, bf16[512,8,128]{2,0,1:T(8,128)(2,1)} %get-tuple-element.103, bf16[512,2,8,128]{3,0,2,1:T(8,128)(2,1)} %bitcast.95, pred[]{:T(512)S(6)} %compare.3), kind=kOutput, calls=%fused_computation.10.clone.1 | convolution fusion | flops 1087373312 | bytes 7340033 | tf_op jit(solution)/shard_map/while/body/eval_jaxpr/hqk,khd->qhd/dot_general | solution.py:38
  136.3 2.0 constant_dynamic-slice_fusion.2
  138.3 1.9 copy.23
  140.2 7.4 %bitcast_add_fusion.2 = f32[512,8,128]{0,2,1:T(8,128)} fusion(f32[512,8,128]{0,2,1:T(8,128)} %get-tuple-element.95, bf16[512,8,128]{2,0,1:T(8,128)(2,1)} %get-tuple-element.103, bf16[512,2,8,128]{3,0,2,1:T(8,128)(2,1)} %bitcast.95, pred[]{:T(512)S(6)} %compare.3), kind=kOutput, calls=%fused_computation.10.clone.1 | convolution fusion | flops 1087373312 | bytes 7340033 | tf_op jit(solution)/shard_map/while/body/eval_jaxpr/hqk,khd->qhd/dot_general | solution.py:38
  147.5 3.0 %copy.14 = f32[512,1024]{1,0:T(8,128)} copy(f32[512,1024]{0,1:T(8,128)} %bitcast.101) | data formatting | bytes 4194304 | tf_op jit(solution)/shard_map/reshape | solution.py:43
  150.5 44.0 %reduce-scatter.2.cloned.1.call-done = f32[128,1024]{1,0:T(8,128)} async-done(((f32[512,1024]{1,0:T(8,128)}), f32[128,1024]{1,0:T(8,128)}) %reduce-scatter.2.cloned.1.call-update) | async-done | bytes 524304 | tf_op jit(solution)/shard_map/reduce_scatter | solution.py:85
  196.9 2.3 %fusion.12 = bf16[128,1024]{1,0:T(8,128)(2,1)} fusion(bf16[1024,1024]{1,0:T(8,128)(2,1)S(1)} %copy-done, bf16[128,1024]{1,0:T(8,128)(2,1)S(1)} %copy-done.3, f32[128,2048]{1,0:T(8,128)S(1)} %fusion.21, f32[128,1024]{1,0:T(8,128)} %reduce-scatter.2.cloned.1.call-done, f32[128]{0:T(128)S(1)} %add_rsqrt_fusion, f32[128]{0:T(128)S(1)} %broadcast_multiply_fusion), kind=kOutput, calls=%fused_computation.21 | convolution fusion | flops 269877248 | bytes 3671040 | tf_op jit(solution)/shard_map/dot_general | solution.py:90
  (39 shorter events, 16.8 us)
Async XLA Ops:
  6.5 190.4 %copy-start = (bf16[1024,1024]{1,0:T(8,128)(2,1)S(1)}, bf16[1024,1024]{1,0:T(8,128)(2,1)}, u32[]{:S(2)}) copy-start(bf16[1024,1024]{1,0:T(8,128)(2,1)} %param.13) | copy-start | bytes 6291460
  6.5 105.7 %all-gather.2.cloned.1.call-start = ((), (), s32[]{:S(2)}) async-start(), calls=%async_computation.1 | async-start | bytes 1310720 | tf_op jit(solution)/shard_map/all_gather | solution.py:84
  18.8 12.6 %copy-start.1 = (bf16[1024,2048]{1,0:T(8,128)(2,1)S(1)}, bf16[1024,2048]{1,0:T(8,128)(2,1)}, u32[]{:S(2)}) copy-start(bf16[1024,2048]{1,0:T(8,128)(2,1)} %param.12) | copy-start | bytes 12582916
  18.8 12.6 %copy-start.2 = (bf16[128,1024]{1,0:T(8,128)(2,1)S(1)}, bf16[128,1024]{1,0:T(8,128)(2,1)}, u32[]{:S(2)}) copy-start(bf16[128,1024]{1,0:T(8,128)(2,1)} %param.10) | copy-start | bytes 786436
  22.5 12.4 %collective-permute-start = (bf16[1,12,16,1024]{3,2,1,0:T(8,128)(2,1)}, bf16[1,12,16,1024]{3,2,1,0:T(8,128)(2,1)}, u32[]{:S(2)}, u32[]{:S(2)}) collective-permute-start(bf16[1,12,16,1024]{3,2,1,0:T(8,128)(2,1)} %get-tuple-element.61), channel_id=1, source_target_pairs={{0,4},{4,0},{8,12},{12,8},{16,20},{20,16},{24,28},{28,24},{1,5},{5... | collective-permute-start | bytes 1179656 | tf_op jit(solution)/shard_map/ppermute | solution.py:70
  25.5 28.2 %collective-permute-start.1 = (bf16[1,12,16,1024]{3,2,1,0:T(8,128)(2,1)}, bf16[1,12,16,1024]{3,2,1,0:T(8,128)(2,1)}, u32[]{:S(2)}, u32[]{:S(2)}) collective-permute-start(bf16[1,12,16,1024]{3,2,1,0:T(8,128)(2,1)} %get-tuple-element.60), channel_id=1, source_target_pairs={{0,8},{4,12},{8,0},{12,4},{16,24},{20,28},{24,16},{28,20},{1,9},{5... | collective-permute-start | bytes 1179656 | tf_op jit(solution)/shard_map/ppermute | solution.py:70
  27.0 32.8 %collective-permute-start.2 = (bf16[1,12,16,1024]{3,2,1,0:T(8,128)(2,1)}, bf16[1,12,16,1024]{3,2,1,0:T(8,128)(2,1)}, u32[]{:S(2)}, u32[]{:S(2)}) collective-permute-start(bf16[1,12,16,1024]{3,2,1,0:T(8,128)(2,1)} %get-tuple-element.59), channel_id=1, source_target_pairs={{0,12},{4,8},{8,4},{12,0},{16,28},{20,24},{24,20},{28,16},{1,13},{... | collective-permute-start | bytes 1179656 | tf_op jit(solution)/shard_map/ppermute | solution.py:70
  27.0 34.6 %collective-permute-start.3 = (bf16[1,12,16,1024]{3,2,1,0:T(8,128)(2,1)}, bf16[1,12,16,1024]{3,2,1,0:T(8,128)(2,1)}, u32[]{:S(2)}, u32[]{:S(2)}) collective-permute-start(bf16[1,12,16,1024]{3,2,1,0:T(8,128)(2,1)} %get-tuple-element.58), channel_id=1, source_target_pairs={{0,16},{4,20},{8,24},{12,28},{16,0},{20,4},{24,8},{28,12},{1,17},{... | collective-permute-start | bytes 1179656 | tf_op jit(solution)/shard_map/ppermute | solution.py:70
  30.0 53.6 %collective-permute-start.4 = (bf16[1,12,16,1024]{3,2,1,0:T(8,128)(2,1)}, bf16[1,12,16,1024]{3,2,1,0:T(8,128)(2,1)S(1)}, u32[]{:S(2)}, u32[]{:S(2)}) collective-permute-start(bf16[1,12,16,1024]{3,2,1,0:T(8,128)(2,1)} %get-tuple-element.57), channel_id=1, source_target_pairs={{0,20},{4,16},{8,28},{12,24},{16,4},{20,0},{24,12},{28,8},{1,21},{... | collective-permute-start | bytes 1179656 | tf_op jit(solution)/shard_map/ppermute | solution.py:70
  32.9 161.6 %reduce-scatter.2.cloned.1.call-start = ((), (), s32[]{:S(2)}) async-start(), calls=%async_computation.2 | async-start | bytes 2621440 | tf_op jit(solution)/shard_map/reduce_scatter | solution.py:85
  34.9 49.6 %collective-permute-start.5 = (bf16[1,12,16,1024]{3,2,1,0:T(8,128)(2,1)}, bf16[1,12,16,1024]{3,2,1,0:T(8,128)(2,1)S(1)}, u32[]{:S(2)}, u32[]{:S(2)}) collective-permute-start(bf16[1,12,16,1024]{3,2,1,0:T(8,128)(2,1)} %get-tuple-element.56), channel_id=1, source_target_pairs={{0,24},{4,28},{8,16},{12,20},{16,8},{20,12},{24,0},{28,4},{1,25},{... | collective-permute-start | bytes 1179656 | tf_op jit(solution)/shard_map/ppermute | solution.py:70
  53.7 31.5 %collective-permute-start.6 = (bf16[1,12,16,1024]{3,2,1,0:T(8,128)(2,1)}, bf16[1,12,16,1024]{3,2,1,0:T(8,128)(2,1)S(1)}, u32[]{:S(2)}, u32[]{:S(2)}) collective-permute-start(bf16[1,12,16,1024]{3,2,1,0:T(8,128)(2,1)} %get-tuple-element.55), channel_id=1, source_target_pairs={{0,28},{4,24},{8,20},{12,16},{16,12},{20,8},{24,4},{28,0},{1,29},{... | collective-permute-start | bytes 1179656 | tf_op jit(solution)/shard_map/ppermute | solution.py:70
  147.5 49.4 %copy-start.3 = (bf16[128,1024]{1,0:T(8,128)(2,1)S(1)}, bf16[128,1024]{1,0:T(8,128)(2,1)}, u32[]{:S(2)}) copy-start(bf16[128,1024]{1,0:T(8,128)(2,1)} %param.10) | copy-start | bytes 786436
Sparse Core Ops, SparseCore 0:
  33.0 16.9 all-gather.1
  150.6 43.8 reduce-scatter.1
